TPU v7x, 32 devices: a whole 2x2x4 slice. The times are simulated.
32 devices in a mesh: wide: 16 (over z, y, core), narrow: 2 (over x).
Axes of the slice: x: 2, y: 2, z: 4, core: 2. Of those that a mesh axis runs over, the one named last changes fastest.
Arguments:
- shocks: bfloat16 [64, 4096], replicated, may hold values from -6 to 6
- load_tiles: bfloat16 [32, 128, 128], P('narrow'), may hold values from -0.5 to 0.5
- load_index: int32 [32, 2], P('narrow'), may hold values from 0 to 31, as said below
- delta_tiles: bfloat16 [1024, 128, 128], P('wide'), may hold values from -0.09375 to 0.09375
- delta_index: int32 [256, 4], P('wide'), may hold values from 0 to 31, all different within a row
- base_value: float32 [32768], P('wide'), may hold values from -3 to 3
- trade_set: int32 [32768], P('wide'), may hold values from 0 to 2047, as said below
- set_slot: int32 [2048], replicated, may hold values from 0 to 2047, as said below
- default_step: int32 [64, 2048], P('narrow', 'wide'), may hold values from 0 to 7
Outputs:
- epe: float32 [2048], P('wide')
- default_loss: float32 [2048], P('wide')
Inputs may be any that keep to these rules, and one draw needn't show every extreme that they name: load_index[i] = (row block, column block); the column blocks of the tiles of narrow index j lie in j * 16 to (j + 1) * 16 - 1, and no pair repeats. `delta_index`: the 4 factor blocks of one trade block differ. `set_slot`: A permutation of the netting sets. `trade_set`: of the 2048 trades of one index of wide, at most 256 have sets of one owner (set_slot // 128); one owner gets exactly 256 from every index of wide.
All inputs are finite; a program needn't handle non-finite values.
Results may differ from a plain program's by a relative error of at most 0.00046.
Values may be sent and summed in bfloat16 or wider, within the bound.
A program may use at most 64 MiB of HBM per device.

v0:
```python
import jax
import jax.numpy as jnp
from jax import lax
from jax.sharding import PartitionSpec as P

BLOCK = 128
STEPS = 8
STEP = 3


def on_device(
    shocks,
    load_tiles,
    load_index,
    delta_tiles,
    delta_index,
    base_value,
    trade_set,
    set_slot,
    default_step,
):
    narrow_count = lax.axis_size("narrow")
    group = lax.axis_index("narrow")
    scen_total, width = shocks.shape
    blocks_all = width // BLOCK
    own_blocks = blocks_all // narrow_count
    shock_blocks = shocks.reshape(scen_total, blocks_all, BLOCK)
    picked = jnp.take(shock_blocks, load_index[:, 0], axis=1)
    loaded = jnp.einsum("sla,lab->slb", picked, load_tiles, preferred_element_type=jnp.float32)
    target = load_index[:, 1] - group * own_blocks
    placing = (target[:, None] == jnp.arange(own_blocks, dtype=jnp.int32)[None, :]).astype(
        jnp.float32
    )
    spread = jnp.einsum("slb,lc->scb", loaded, placing, precision=lax.Precision.HIGHEST)
    own_columns = lax.dynamic_slice_in_dim(shock_blocks, group * own_blocks, own_blocks, 1).astype(
        jnp.float32
    )
    moves_own = (own_columns + spread).astype(jnp.bfloat16).reshape(scen_total, own_blocks * BLOCK)
    moves = lax.all_to_all(moves_own, "narrow", split_axis=0, concat_axis=1, tiled=True)
    scen_dev = moves.shape[0]
    move_blocks = moves.reshape(scen_dev, blocks_all, BLOCK)
    tb_count, per_block = delta_index.shape
    gathered = jnp.take(move_blocks, delta_index.reshape(-1), axis=1).reshape(
        scen_dev, tb_count, per_block, BLOCK
    )
    tile_groups = delta_tiles.reshape(tb_count, per_block, BLOCK, BLOCK)
    valued = jnp.einsum("sbka,bkat->sbt", gathered, tile_groups, preferred_element_type=jnp.float32)
    values = valued.reshape(scen_dev, tb_count * BLOCK) + base_value[None, :]
    wide_count = lax.axis_size("wide")
    own_sets = default_step.shape[1]
    slots = jnp.take(set_slot, trade_set)
    owner = slots // own_sets
    local = slots % own_sets
    capacity = 2 * trade_set.shape[0] // wide_count
    owner_hits = (owner[:, None] == jnp.arange(wide_count, dtype=jnp.int32)[None, :]).astype(
        jnp.int32
    )
    position = jnp.sum(jnp.cumsum(owner_hits, axis=0) * owner_hits, axis=1) - 1
    target_slot = owner * capacity + position
    sent_values = (
        jnp.zeros((scen_dev, wide_count * capacity), jnp.float32).at[:, target_slot].set(values)
    )
    sent_ids = (
        jnp.full((1, wide_count * capacity), float(own_sets), jnp.float32)
        .at[0, target_slot]
        .set(local.astype(jnp.float32))
    )
    got_values, got_ids = (
        lax.all_to_all(sent_values, "wide", split_axis=1, concat_axis=1, tiled=True),
        lax.all_to_all(sent_ids, "wide", split_axis=1, concat_axis=1, tiled=True),
    )
    member = (got_ids[0][None, :] == jnp.arange(own_sets, dtype=jnp.float32)[:, None]).astype(
        jnp.float32
    )
    netted = jnp.einsum("sr,nr->sn", got_values, member, precision=lax.Precision.HIGHEST)
    exposure = jnp.maximum(netted, 0.0)
    default_hit = (default_step == STEP).astype(jnp.float32)
    totals = lax.psum(
        (jnp.sum(exposure, axis=0), jnp.sum(default_hit * exposure, axis=0)), "narrow"
    )
    scen_all = scen_dev * narrow_count
    return (totals[0] / scen_all, totals[1] * (STEPS / scen_all))


def solution(mesh):
    return jax.shard_map(
        on_device,
        mesh=mesh,
        in_specs=(
            P(),
            P("narrow", None, None),
            P("narrow", None),
            P("wide", None, None),
            P("wide", None),
            P("wide"),
            P("wide"),
            P(),
            P("narrow", "wide"),
        ),
        out_specs=(P("wide"), P("wide")),
        check_vma=False,
    )
```

profile of v0, /device:TPU:0, one launch (start us, length us, event | category | flops | bytes accessed | tf_op | source)
XLA Modules:
  0.0 80.2 jit_solution(11723574881305017320)
XLA Ops:
  0.6 0.0 copy-start
  0.6 1.3 %copy_bitcast_fusion = bf16[64,32,128]{2,0,1:T(8,128)(2,1)S(1)} fusion(bf16[64,4096]{1,0:T(8,128)(2,1)} %param.9), kind=kLoop, calls=%fused_computation.16 | loop fusion | bytes 1048576 | tf_op jit(solution)/shard_map/reshape | solution.py:27
  2.0 0.7 and_bitcast_fusion
  2.7 0.8 subtract_bitcast_fusion
  3.4 1.1 %copy.44 = bf16[8,8,32,128]{3,2,1,0:T(8,128)(2,1)S(1)} copy(bf16[8,8,32,128]{3,1,2,0:T(8,128)(2,1)} %bitcast.73) | data formatting | bytes 1048576
  4.6 0.0 copy-start.4
  4.6 0.0 copy-start.2
  4.6 0.0 copy-start.1
  4.6 0.6 gather_fusion.1
  5.2 1.4 %convolution_bitcast_fusion.1 = f32[64,16,128]{2,0,1:T(8,128)S(1)} fusion(bf16[16,128,128]{2,1,0:T(8,128)(2,1)} %param.10, bf16[16,64,128]{2,1,0:T(8,128)(2,1)S(1)} %gather_fusion.1, pred[16]{0:T(512)(128)(4,1)S(1)} %and_bitcast_fusion), kind=kOutput, calls=%fused_computation.9 | convolution fusion | flops 33685504 | bytes 1310736 | tf_op jit(solution)/shard_map/sla,lab->slb/dot_general | solution.py:29
  6.6 0.7 fusion.2
  7.3 0.8 %all_to_all.26 = bf16[2,32,2048]{2,1,0:T(8,128)(2,1)} reshape(bf16[64,16,128]{2,1,0:T(8,128)(2,1)S(1)} %fusion.2) | data formatting | bytes 524288 | tf_op jit(solution)/shard_map/all_to_all | solution.py:39
  8.1 4.2 %all-to-all-start = ((bf16[2,32,2048]{2,1,0:T(8,128)(2,1)}), bf16[2,32,2048]{2,1,0:T(8,128)(2,1)S(1)}, u32[]{:S(2)}, u32[]{:S(2)}) async-start(bf16[2,32,2048]{2,1,0:T(8,128)(2,1)} %all_to_all.26), calls=%async_computation | async-start | bytes 524288 | tf_op jit(solution)/shard_map/all_to_all | solution.py:39
  12.3 0.0 copy-done.4
  12.3 0.1 copy.33
  12.4 0.0 copy-done.2
  12.4 0.0 copy-done.1
  12.5 11.8 %gather_fusion = s32[2048]{0:T(1024)S(1)} fusion(s32[2048]{0:T(1024)S(1)} %copy-done.1, s32[2048]{0:T(1024)S(1)} %fusion.26), kind=kCustom, calls=%fused_computation | custom fusion | bytes 24576 | tf_op jit(solution)/shard_map/jit(_take)/gather | solution.py:51
  24.3 4.5 %reduce-window.6 = s32[16,16,128]{2,1,0:T(8,128)S(1)} reduce-window(s32[16,16,128]{2,1,0:T(8,128)S(1)} %fusion.18, s32[]{:T(128)} %constant.84.clone.1), window={size=1x1x128 pad=0_0x0_0x127_0}, to_apply=%region_0.1 | reduce-window | flops 4161536 | bytes 262148 | tf_op jit(solution)/shard_map/reduce-window
  28.8 0.4 slice_reduce_fusion
  29.3 0.2 reduce-window.9
  29.4 0.1 broadcast_add_fusion
  29.6 0.1 fusion.16
  29.6 0.1 reshape.123
  29.7 0.1 copy.29
  29.8 0.0 all-to-all-done
  29.8 0.3 copy.32
  30.1 0.2 reshape.122
  30.3 0.1 copy.34
  30.4 0.0 copy-start.3
  30.4 0.7 gather_fusion.2
  31.1 0.0 copy-done
  31.1 0.5 convolution_bitcast_fusion.2
  31.6 0.3 copy.36
  31.9 7.0 %scatter_custom_fusion = f32[32,4096]{0,1:T(8,128)} fusion(s32[2048]{0:T(1024)S(1)} %compare_select_fusion, f32[2048,32]{1,0:T(8,128)S(1)} %copy.36, f32[]{:T(128)} %constant.64.clone.1), kind=kCustom, calls=%fused_computation.14 | custom fusion | bytes 524292 | tf_op jit(solution)/shard_map/scatter | solution.py:61
  39.0 3.0 %copy.37 = f32[32,16,256]{2,0,1:T(8,128)} copy(f32[32,16,256]{0,2,1:T(8,128)} %bitcast.71) | data formatting | bytes 1048576 | tf_op jit(solution)/shard_map/all_to_all | solution.py:69
  42.0 6.6 %all-to-all-start.1 = ((f32[32,16,256]{2,0,1:T(8,128)}), f32[32,16,256]{2,0,1:T(8,128)S(1)}, u32[]{:S(2)}, u32[]{:S(2)}) async-start(f32[32,16,256]{2,0,1:T(8,128)} %copy.37), calls=%async_computation.1 | async-start | bytes 1048576 | tf_op jit(solution)/shard_map/all_to_all | solution.py:69
  48.6 0.0 copy-done.5
  48.6 0.1 fusion.19
  48.7 0.0 copy-done.6
  48.7 0.1 and_reduce_fusion
  48.9 8.6 %scatter_custom_fusion.1 = f32[4096]{0:T(1024)} fusion(s32[2048]{0:T(1024)S(1)} %broadcast_select_fusion, f32[2048]{0:T(1024)S(1)} %get-tuple-element.6, f32[]{:T(128)} %constant.99.clone.1), kind=kCustom, calls=%fused_computation.47 | custom fusion | bytes 16388
  57.5 5.4 %all-to-all-done.1 = f32[32,16,256]{2,0,1:T(8,128)S(1)} async-done(((f32[32,16,256]{2,0,1:T(8,128)}), f32[32,16,256]{2,0,1:T(8,128)S(1)}, u32[]{:S(2)}, u32[]{:S(2)}) %all-to-all-start.1) | async-done | bytes 524320 | tf_op jit(solution)/shard_map/all_to_all | solution.py:69
  62.9 4.2 %all-to-all-start.2 = ((f32[1,16,256]{2,0,1:T(1,128)}), f32[1,16,256]{2,0,1:T(1,128)S(1)}, u32[]{:S(2)}, u32[]{:S(2)}) async-start(f32[1,16,256]{2,0,1:T(1,128)} %bitcast.20), calls=%async_computation.2 | async-start | bytes 32768 | tf_op jit(solution)/shard_map/all_to_all | solution.py:70
  67.1 6.5 %all-to-all-done.2 = f32[1,16,256]{2,0,1:T(1,128)S(1)} async-done(((f32[1,16,256]{2,0,1:T(1,128)}), f32[1,16,256]{2,0,1:T(1,128)S(1)}, u32[]{:S(2)}, u32[]{:S(2)}) %all-to-all-start.2) | async-done | bytes 16416 | tf_op jit(solution)/shard_map/all_to_all | solution.py:70
  73.6 1.2 %select_reduce_fusion = (f32[128]{0:T(128)S(1)}, f32[128]{0:T(128)S(1)}) fusion(s32[32,128]{1,0:T(8,128)S(1)} %copy-done.7, f32[32,4096]{1,0:T(8,128)S(1)} %bitcast.77, f32[4096]{0:T(1024)S(1)} %bitcast.83), kind=kOutput, calls=%fused_computation.40 | convolution fusion | flops 201871104 | bytes 558080 | tf_op jit(solution)/shard_map/sr,nr->sn/dot_general | solution.py:75
  74.8 4.9 %all-reduce.1 = (f32[128]{0:T(128)S(1)}, f32[128]{0:T(128)S(1)}) all-reduce(f32[128]{0:T(128)S(1)} %get-tuple-element.3, f32[128]{0:T(128)S(1)} %get-tuple-element.2), channel_id=1, replica_groups=mesh['wide'=16,'narrow'=2] {'narrow'}, use_global_device_ids=true, to_apply=%region_6.7 | all-reduce | flops 256 | bytes 2048 | tf_op jit(solution)/shard_map/psum | solution.py:78
  79.7 0.5 broadcast_multiply_fusion
  (16 shorter events, 0.1 us)
Async XLA Ops:
  0.6 30.5 %copy-start = (bf16[64,128,128]{2,1,0:T(8,128)(2,1)S(1)}, bf16[64,128,128]{2,1,0:T(8,128)(2,1)}, u32[]{:S(2)}) copy-start(bf16[64,128,128]{2,1,0:T(8,128)(2,1)} %param.12) | copy-start | bytes 6291460
  4.6 7.8 %copy-start.4 = (s32[16,4]{0,1:T(4,128)S(1)}, s32[16,4]{0,1:T(4,128)}, u32[]{:S(2)}) copy-start(s32[16,4]{0,1:T(4,128)} %param.13) | copy-start | bytes 772
  4.6 7.8 %copy-start.2 = (s32[2048]{0:T(1024)S(1)}, s32[2048]{0:T(1024)}, u32[]{:S(2)}) copy-start(s32[2048]{0:T(1024)} %param.15) | copy-start | bytes 24580
  4.6 7.8 %copy-start.1 = (s32[2048]{0:T(1024)S(1)}, s32[2048]{0:T(1024)}, u32[]{:S(2)}) copy-start(s32[2048]{0:T(1024)} %param.16) | copy-start | bytes 24580
  8.1 21.7 %all-to-all-start = ((bf16[2,32,2048]{2,1,0:T(8,128)(2,1)}), bf16[2,32,2048]{2,1,0:T(8,128)(2,1)S(1)}, u32[]{:S(2)}, u32[]{:S(2)}) async-start(bf16[2,32,2048]{2,1,0:T(8,128)(2,1)} %all_to_all.26), calls=%async_computation | async-start | bytes 524288 | tf_op jit(solution)/shard_map/all_to_all | solution.py:39
  30.4 1.2 %copy-start.3 = (f32[2048]{0:T(1024)S(1)}, f32[2048]{0:T(1024)}, u32[]{:S(2)}) copy-start(f32[2048]{0:T(1024)} %param.14) | copy-start | bytes 24580
  39.0 9.7 %copy-start.5 = (s32[2]{0:T(128)S(1)}, s32[2]{0:T(128)}, u32[]{:S(2)}) copy-start(s32[2]{0:T(128)} %constant.106) | copy-start | bytes 28
  39.0 9.8 %copy-start.6 = (s32[2]{0:T(128)S(1)}, s32[2]{0:T(128)}, u32[]{:S(2)}) copy-start(s32[2]{0:T(128)} %constant.109) | copy-start | bytes 28
  39.0 34.6 %copy-start.7 = (s32[32,128]{1,0:T(8,128)S(1)}, s32[32,128]{1,0:T(8,128)}, u32[]{:S(2)}) copy-start(s32[32,128]{1,0:T(8,128)} %param.17) | copy-start | bytes 49156
  42.0 20.9 %all-to-all-start.1 = ((f32[32,16,256]{2,0,1:T(8,128)}), f32[32,16,256]{2,0,1:T(8,128)S(1)}, u32[]{:S(2)}, u32[]{:S(2)}) async-start(f32[32,16,256]{2,0,1:T(8,128)} %copy.37), calls=%async_computation.1 | async-start | bytes 1048576 | tf_op jit(solution)/shard_map/all_to_all | solution.py:69
  62.9 10.7 %all-to-all-start.2 = ((f32[1,16,256]{2,0,1:T(1,128)}), f32[1,16,256]{2,0,1:T(1,128)S(1)}, u32[]{:S(2)}, u32[]{:S(2)}) async-start(f32[1,16,256]{2,0,1:T(1,128)} %bitcast.20), calls=%async_computation.2 | async-start | bytes 32768 | tf_op jit(solution)/shard_map/all_to_all | solution.py:70
where the time goes:
time: 80.7 us; the launch traced here: 80.2 us
  local copies, waits for them, and re-layouts  36.6 us (45%)
  starting transfers between devices  15 us (19%)
  waiting for transfers between devices  11.9 us (15%)
  other arithmetic  7.14 us (9%)
  blocking collectives  4.93 us (6%)
  matrix products  3.71 us (5%)
  between operations  0.91 us (1%)
    gather x1, local copies, waits for them, and re-layouts, on_device(): slots = jnp.take(set_slot, trade_set)  11.8 us
    unnamed x19, local copies, waits for them, and re-layouts  9.88 us
    scatter x1, local copies, waits for them, and re-layouts, on_device(): jnp.zeros((scen_dev, wide_count * capacity), jnp.float32).at[:, target_slot]  7.03 us
    all_to_all x1, starting transfers between devices, on_device(): lax.all_to_all(sent_values, 'wide', split_axis=1, concat_axis=1, tiled=True)  6.63 us
    all_to_all x1, waiting for transfers between devices, on_device(): lax.all_to_all(sent_ids, 'wide', split_axis=1, concat_axis=1, tiled=True)  6.45 us
    all_to_all x1, waiting for transfers between devices, on_device(): lax.all_to_all(sent_values, 'wide', split_axis=1, concat_axis=1, tiled=True)  5.43 us
    psum x1, blocking collectives, on_device(): lax.psum((jnp.sum(exposure, axis=0), jnp.sum(default_hit * exposure, axis...  4.93 us
    another operation x3, other arithmetic  4.82 us
  transfers between devices with their start and end apart: 3, of which 2 were waited for; matrix products, arithmetic and copies ran while one was open for 33% of the time, Pallas kernels for 0%

commit v1 on v0

v1 whole, which is shorter than its diff:
```python
import functools

import jax
import jax.numpy as jnp
from jax import lax
from jax.experimental import pallas as pl
from jax.experimental.pallas import tpu as pltpu
from jax.sharding import PartitionSpec as P

BLOCK = 128
STEPS = 8
STEP = 3
MESH = pl.DeviceIdType.MESH
F32 = jnp.float32
BF16 = jnp.bfloat16


def one_hot(row, size):
    lane = lax.broadcasted_iota(jnp.int32, (size, row.shape[1]), 0)
    return jnp.where(lane == row, 1.0, 0.0)


def kernel(
    narrow_count,
    wide_count,
    shocks,
    load_tiles,
    load_index,
    delta_tiles,
    delta_index,
    base,
    trade_set,
    set_slot,
    default_step,
    epe,
    default_loss,
    shock_blocks,
    moves_out,
    moves,
    parts,
    deltas,
    member,
    pair_mask,
    high,
    low,
    partial,
    got_pair,
    halved,
    got_wide,
    sums,
    delta_sem,
    move_send,
    move_recv,
    pair_send,
    pair_recv,
    wide_send,
    wide_recv,
    sum_send,
    sum_recv,
):
    group = lax.axis_index("narrow")
    wide = lax.axis_index("wide")
    couples = wide_count // 2
    couple = wide // 2
    parity = lax.rem(wide, 2)
    scen_all = shocks.shape[0]
    own_blocks = moves_out.shape[1]
    scen_dev = moves.shape[1]
    tiles = load_tiles.shape[0]
    trade_blocks, per_block = delta_index.shape
    own_sets = default_step.shape[1]
    span = 2 * own_sets
    bits = span.bit_length() - 1

    fetch = pltpu.make_async_copy(delta_tiles, deltas, delta_sem)
    fetch.start()
    narrow_peers = [lax.rem(group + k, narrow_count) for k in range(1, narrow_count)]
    wide_peers = [lax.rem(couple + k, couples) * 2 + parity for k in range(1, couples)]
    partner = couple * 2 + 1 - parity
    barrier = pltpu.get_barrier_semaphore()
    for peer in narrow_peers:
        pl.semaphore_signal(barrier, inc=1, device_id={"narrow": peer}, device_id_type=MESH)
    for peer in wide_peers + [partner]:
        pl.semaphore_signal(barrier, inc=1, device_id={"wide": peer}, device_id_type=MESH)

    for c in range(shock_blocks.shape[0]):
        shock_blocks[c] = shocks[:, c * BLOCK : (c + 1) * BLOCK]
    for i in range(tiles):
        parts[i] = jnp.dot(
            shock_blocks[load_index[i, 0]], load_tiles[i], preferred_element_type=F32
        )
    columns = [jnp.full((1, BLOCK), load_index[i, 1]) for i in range(tiles)]
    for c in range(own_blocks):
        column = group * own_blocks + c
        total = shock_blocks[column].astype(F32)
        for i in range(tiles):
            total += parts[i] * jnp.where(columns[i] == column, 1.0, 0.0)
        rounded = total.astype(BF16)
        for n in range(narrow_count):
            moves_out[n, c] = rounded[n * scen_dev : (n + 1) * scen_dev]

    pl.semaphore_wait(barrier, len(narrow_peers) + len(wide_peers) + 1)
    own_rows = pl.ds(group * own_blocks, own_blocks)
    move_copies = [
        pltpu.make_async_remote_copy(
            src_ref=moves_out.at[peer],
            dst_ref=moves.at[own_rows],
            send_sem=move_send.at[k],
            recv_sem=move_recv.at[k],
            device_id={"narrow": peer},
            device_id_type=MESH,
        )
        for k, peer in enumerate(narrow_peers)
    ]
    for copy in move_copies:
        copy.start()
    moves[own_rows] = moves_out[group]

    slots = set_slot[...]
    digits = jnp.concatenate(
        [lax.shift_right_logical(slots, bits), lax.bitwise_and(slots, span - 1)], axis=0
    )
    table = digits.astype(F32).astype(BF16)
    set_rows = slots.shape[0]
    for b in range(trade_blocks):
        ids = trade_set[b : b + 1, :]
        low_hot = one_hot(lax.bitwise_and(ids, BLOCK - 1), BLOCK).astype(BF16)
        looked = jnp.dot(table, low_hot, preferred_element_type=F32)
        row_hot = one_hot(lax.shift_right_logical(ids, 7), set_rows)
        upper = jnp.sum(looked[:set_rows] * row_hot, axis=0, keepdims=True)
        lower = jnp.sum(looked[set_rows:] * row_hot, axis=0, keepdims=True)
        lanes = slice(b * BLOCK, (b + 1) * BLOCK)
        member[:, lanes] = one_hot(lower.astype(jnp.int32), span).astype(BF16)
        spread = jnp.broadcast_to(upper, (scen_dev, BLOCK))
        for e in range(couples):
            pair_mask[e * scen_dev : (e + 1) * scen_dev, lanes] = jnp.where(
                spread == float(e), 1.0, 0.0
            ).astype(BF16)

    for copy in move_copies:
        copy.wait()
    fetch.wait()

    for b in range(trade_blocks):
        picked = jnp.concatenate(
            [moves[delta_index[b, k]] for k in range(per_block)], axis=1
        )
        block = deltas[b * per_block : (b + 1) * per_block].reshape(per_block * BLOCK, BLOCK)
        value = jnp.dot(picked, block, preferred_element_type=F32) + base[b : b + 1, :]
        first = value.astype(BF16)
        second = (value - first.astype(F32)).astype(BF16)
        lanes = slice(b * BLOCK, (b + 1) * BLOCK)
        for e in range(couples):
            rows = slice(e * scen_dev, (e + 1) * scen_dev)
            mask = pair_mask[rows, lanes]
            high[rows, lanes] = first * mask
            low[rows, lanes] = second * mask
    contract = (((1,), (1,)), ((), ()))
    hot = member[...]
    netted = lax.dot_general(
        high[...], hot, contract, preferred_element_type=F32
    ) + lax.dot_general(low[...], hot, contract, preferred_element_type=F32)
    for e in range(couples):
        rows = slice(e * scen_dev, (e + 1) * scen_dev)
        partial[0, e] = netted[rows, :own_sets]
        partial[1, e] = netted[rows, own_sets:]

    swap = pltpu.make_async_remote_copy(
        src_ref=partial.at[1 - parity],
        dst_ref=got_pair,
        send_sem=pair_send,
        recv_sem=pair_recv,
        device_id={"wide": partner},
        device_id_type=MESH,
    )
    swap.start()
    swap.wait()
    halved[...] = partial[parity] + got_pair[...]
    wide_copies = [
        pltpu.make_async_remote_copy(
            src_ref=halved.at[lax.rem(couple + k + 1, couples)],
            dst_ref=got_wide.at[k],
            send_sem=wide_send.at[k],
            recv_sem=wide_recv.at[k],
            device_id={"wide": peer},
            device_id_type=MESH,
        )
        for k, peer in enumerate(wide_peers)
    ]
    for copy in wide_copies:
        copy.start()
    for copy in wide_copies:
        copy.wait()
    total = halved[couple]
    for k in range(len(wide_peers)):
        total += got_wide[k]

    exposure = jnp.maximum(total, 0.0)
    hit = jnp.where(default_step[...] == STEP, exposure, 0.0)
    sums[group, 0:1] = jnp.sum(exposure, axis=0, keepdims=True)
    sums[group, 1:2] = jnp.sum(hit, axis=0, keepdims=True)
    sum_copies = [
        pltpu.make_async_remote_copy(
            src_ref=sums.at[group],
            dst_ref=sums.at[group],
            send_sem=sum_send.at[k],
            recv_sem=sum_recv.at[k],
            device_id={"narrow": peer},
            device_id_type=MESH,
        )
        for k, peer in enumerate(narrow_peers)
    ]
    for copy in sum_copies:
        copy.start()
    for copy in sum_copies:
        copy.wait()
    both = sums[0]
    for n in range(1, narrow_count):
        both += sums[n]
    epe[...] = both[0:1] * (1.0 / scen_all)
    default_loss[...] = both[1:2] * (STEPS / scen_all)


def on_device(
    shocks,
    load_tiles,
    load_index,
    delta_tiles,
    delta_index,
    base_value,
    trade_set,
    set_slot,
    default_step,
):
    narrow_count = lax.axis_size("narrow")
    wide_count = lax.axis_size("wide")
    scen_all, width = shocks.shape
    factor_blocks = width // BLOCK
    own_blocks = factor_blocks // narrow_count
    scen_dev, own_sets = default_step.shape
    trades = trade_set.shape[0]
    couples = wide_count // 2
    lines = couples * scen_dev
    vmem = pl.BlockSpec(memory_space=pltpu.VMEM)
    smem = pl.BlockSpec(memory_space=pltpu.SMEM)
    dma = pltpu.SemaphoreType.DMA
    epe, default_loss = pl.pallas_call(
        functools.partial(kernel, narrow_count, wide_count),
        out_shape=(jax.ShapeDtypeStruct((1, own_sets), F32),) * 2,
        in_specs=[
            vmem,
            vmem,
            smem,
            pl.BlockSpec(memory_space=pl.ANY),
            smem,
            vmem,
            vmem,
            vmem,
            vmem,
        ],
        out_specs=(vmem, vmem),
        scratch_shapes=[
            pltpu.VMEM((factor_blocks, scen_all, BLOCK), BF16),
            pltpu.VMEM((narrow_count, own_blocks, scen_dev, BLOCK), BF16),
            pltpu.VMEM((factor_blocks, scen_dev, BLOCK), BF16),
            pltpu.VMEM((load_tiles.shape[0], scen_all, BLOCK), F32),
            pltpu.VMEM(delta_tiles.shape, BF16),
            pltpu.VMEM((2 * own_sets, trades), BF16),
            pltpu.VMEM((lines, trades), BF16),
            pltpu.VMEM((lines, trades), BF16),
            pltpu.VMEM((lines, trades), BF16),
            pltpu.VMEM((2, couples, scen_dev, own_sets), F32),
            pltpu.VMEM((couples, scen_dev, own_sets), F32),
            pltpu.VMEM((couples, scen_dev, own_sets), F32),
            pltpu.VMEM((couples - 1, scen_dev, own_sets), F32),
            pltpu.VMEM((narrow_count, 2, own_sets), F32),
            dma,
            dma((narrow_count - 1,)),
            dma((narrow_count - 1,)),
            dma,
            dma,
            dma((couples - 1,)),
            dma((couples - 1,)),
            dma((narrow_count - 1,)),
            dma((narrow_count - 1,)),
        ],
        compiler_params=pltpu.CompilerParams(collective_id=0, has_side_effects=True),
    )(
        shocks,
        load_tiles,
        load_index,
        delta_tiles,
        delta_index,
        base_value.reshape(-1, BLOCK),
        trade_set.reshape(-1, BLOCK),
        set_slot.reshape(-1, BLOCK),
        default_step,
    )
    return epe.reshape(-1), default_loss.reshape(-1)


def solution(mesh):
    return jax.shard_map(
        on_device,
        mesh=mesh,
        in_specs=(
            P(),
            P("narrow", None, None),
            P("narrow", None),
            P("wide", None, None),
            P("wide", None),
            P("wide"),
            P("wide"),
            P(),
            P("narrow", "wide"),
        ),
        out_specs=(P("wide"), P("wide")),
        check_vma=False,
    )
```

time: 80.7 us -> 26.7 us (0.33)
  local copies, waits for them, and re-layouts: 36.6 us -> 5.01 us
  Pallas kernels: 0 us -> 20.8 us
  starting transfers between devices: 15 us -> 0 us
  waiting for transfers between devices: 11.9 us -> 0 us
  other arithmetic: 7.14 us -> 0 us
  blocking collectives: 4.93 us -> 0 us
  matrix products: 3.71 us -> 0 us
    pallas_call x0 -> x1, Pallas kernels: none -> 20.8 us  [on_device(): pl.pallas_call(functools.partial(kernel, narrow_count, wide_count), out_s...]
    all_to_all x3 -> x0, starting transfers between devices: 15 us -> none  [the longest x1 6.63 us: on_device(): lax.all_to_all(sent_values, 'wide', split_axis=1, concat_axis=1, tiled=True)]
    gather x3 -> x0, local copies, waits for them, and re-layouts: 13 us -> none  [the longest x1 11.8 us: on_device(): slots = jnp.take(set_slot, trade_set)]
    all_to_all x3 -> x0, waiting for transfers between devices: 11.9 us -> none  [the longest x1 6.45 us: on_device(): lax.all_to_all(sent_ids, 'wide', split_axis=1, concat_axis=1, tiled=True)]
    scatter x1 -> x0, local copies, waits for them, and re-layouts: 7.03 us -> none  [on_device(): jnp.zeros((scen_dev, wide_count * capacity), jnp.float32).at[:, target_slot]]
    psum x1 -> x0, blocking collectives: 4.93 us -> none  [on_device(): lax.psum((jnp.sum(exposure, axis=0), jnp.sum(default_hit * exposure, axis...]
    unnamed x19 -> x4, local copies, waits for them, and re-layouts: 9.88 us -> 5.01 us
    another operation x3 -> x0, other arithmetic: 4.82 us -> none
  transfers between devices with their start and end apart: 3 -> 0, of which waited for: 2 -> 0; matrix products, arithmetic and copies ran while one was open for 33% -> 0% of each run, Pallas kernels for 0% -> 0%
where the time goes in v1:
time: 26.7 us; the launch traced here: 26.5 us
  Pallas kernels  20.8 us (78%)
  local copies, waits for them, and re-layouts  5.01 us (19%)
  between operations  0.64 us (2%)
    pallas_call x1, Pallas kernels, on_device(): pl.pallas_call(functools.partial(kernel, narrow_count, wide_count), out_s...  20.8 us
    unnamed x4, local copies, waits for them, and re-layouts  5.01 us

profile of v1, /device:TPU:0, one launch (start us, length us, event | category | flops | bytes accessed | tf_op | source)
XLA Modules:
  0.0 26.5 jit_solution(12086763974819537423)
XLA Ops:
  0.6 1.3 %copy.11.load_index = s32[16,2]{1,0:T(8,128)} copy(s32[16,2]{0,1:T(2,128)} %param.11) | data formatting | bytes 256 | tf_op args[2]
  2.0 1.3 %copy.12.delta_index = s32[16,4]{1,0:T(8,128)} copy(s32[16,4]{0,1:T(4,128)} %param.13) | data formatting | bytes 512 | tf_op args[4]
  3.3 20.8 %shard_map.104 = (f32[1,128]{1,0:T(1,128)}, f32[1,128]{1,0:T(1,128)}) custom-call(bf16[64,4096]{1,0:T(8,128)(2,1)} %shocks.1, bf16[16,128,128]{2,1,0:T(8,128)(2,1)} %load_tiles.1, s32[16,2]{1,0:T(8,128)} %copy.11.load_index, bf16[64,128,128]{2,1,0:T(8,128)(2,1)} %delta_tiles.1, s32[16,4]{1,0:T(8,128)} %copy.12.delta_index, f32[16,128]{1,0:T(8,128)} %bitcast.5, ...), custom_call_target="tpu_custom_call" | custom-call | tf_op jit(solution)/shard_map/pallas_call | solution.py:247
  24.2 1.2 %copy.15 = f32[128]{0:T(128)} copy(f32[128]{0:T(128)} %bitcast.9) | data formatting | bytes 1024
  25.3 1.1 %copy.16 = f32[128]{0:T(128)} copy(f32[128]{0:T(128)} %bitcast.8) | data formatting | bytes 1024

commit v2 on v1

v2 whole, which is shorter than its diff:
```python
import functools

import jax
import jax.numpy as jnp
from jax import lax
from jax.experimental import pallas as pl
from jax.experimental.pallas import tpu as pltpu
from jax.sharding import PartitionSpec as P

BLOCK = 128
STEPS = 8
STEP = 3
MESH = pl.DeviceIdType.MESH
F32 = jnp.float32
BF16 = jnp.bfloat16


def one_hot(row, size):
    lane = lax.broadcasted_iota(jnp.int32, (size, row.shape[1]), 0)
    return jnp.where(lane == row, 1.0, 0.0)


def kernel(
    narrow_count,
    wide_count,
    shocks_hbm,
    load_tiles_hbm,
    load_index_hbm,
    delta_tiles_hbm,
    delta_index_hbm,
    base_hbm,
    trade_set_hbm,
    set_slot_hbm,
    default_step_hbm,
    sums_out,
    shocks,
    load_tiles,
    load_index,
    delta_tiles,
    delta_index,
    base,
    trade_set,
    set_slot,
    default_step,
    shock_blocks,
    moves_out,
    moves,
    parts,
    member,
    pair_mask,
    spread_values,
    partial,
    got_pair,
    halved,
    got_wide,
    sums,
    fetch_sem,
    move_send,
    move_recv,
    pair_send,
    pair_recv,
    wide_send,
    wide_recv,
    sum_send,
    sum_recv,
):
    group = lax.axis_index("narrow")
    wide = lax.axis_index("wide")
    couples = wide_count // 2
    couple = wide // 2
    parity = lax.rem(wide, 2)
    own_blocks = moves_out.shape[1]
    scen_dev = moves.shape[1]
    tiles = load_tiles.shape[0]
    per_block, trade_blocks = delta_index.shape
    own_sets = default_step.shape[1]
    span = 2 * own_sets
    bits = span.bit_length() - 1
    half = couples // 2
    near = couple // half
    place = lax.rem(couple, half)

    narrow_peers = [lax.rem(group + k, narrow_count) for k in range(1, narrow_count)]
    targets = [(0, (1 - near) * half, lax.rem(place + k, half)) for k in range(half)]
    targets += [(1, near * half, lax.rem(place + k, half)) for k in range(1, half)]
    partner = couple * 2 + 1 - parity
    barrier = pltpu.get_barrier_semaphore()
    for _, start, j in targets:
        peer = (start + j) * 2 + parity
        pl.semaphore_signal(barrier, inc=1, device_id={"wide": peer}, device_id_type=MESH)
    for peer in narrow_peers:
        pl.semaphore_signal(barrier, inc=1, device_id={"narrow": peer}, device_id_type=MESH)
    pl.semaphore_signal(barrier, inc=1, device_id={"wide": partner}, device_id_type=MESH)
    fetches = [
        pltpu.make_async_copy(source, target, fetch_sem.at[i])
        for i, (source, target) in enumerate(
            (
                (shocks_hbm, shocks),
                (load_index_hbm, load_index),
                (load_tiles_hbm, load_tiles),
                (trade_set_hbm, trade_set),
                (set_slot_hbm, set_slot),
                (delta_index_hbm, delta_index),
                (delta_tiles_hbm, delta_tiles),
                (base_hbm, base),
                (default_step_hbm, default_step),
            )
        )
    ]
    for fetch in fetches:
        fetch.start()
    for fetch in fetches[:3]:
        fetch.wait()

    for c in range(shock_blocks.shape[0]):
        shock_blocks[c] = shocks[:, c * BLOCK : (c + 1) * BLOCK]
    for i in range(tiles):
        parts[i] = jnp.dot(
            shock_blocks[load_index[0, i]], load_tiles[i], preferred_element_type=F32
        )
    columns = [jnp.full((1, BLOCK), load_index[1, i]) for i in range(tiles)]
    for c in range(own_blocks):
        column = group * own_blocks + c
        total = shock_blocks[column].astype(F32)
        for i in range(tiles):
            total += parts[i] * jnp.where(columns[i] == column, 1.0, 0.0)
        rounded = total.astype(BF16)
        for n in range(narrow_count):
            moves_out[n, c] = rounded[n * scen_dev : (n + 1) * scen_dev]

    pl.semaphore_wait(barrier, len(narrow_peers) + len(targets) + 1)
    own_rows = pl.ds(group * own_blocks, own_blocks)
    move_copies = [
        pltpu.make_async_remote_copy(
            src_ref=moves_out.at[peer],
            dst_ref=moves.at[own_rows],
            send_sem=move_send.at[k],
            recv_sem=move_recv.at[k],
            device_id={"narrow": peer},
            device_id_type=MESH,
        )
        for k, peer in enumerate(narrow_peers)
    ]
    for copy in move_copies:
        copy.start()
    moves[own_rows] = moves_out[group]

    for fetch in fetches[3:]:
        fetch.wait()
    slots = set_slot[...]
    digits = jnp.concatenate(
        [lax.shift_right_logical(slots, bits), lax.bitwise_and(slots, span - 1)], axis=0
    )
    table = digits.astype(F32).astype(BF16)
    set_rows = slots.shape[0]
    for b in range(trade_blocks):
        ids = trade_set[b : b + 1, :]
        low_hot = one_hot(lax.bitwise_and(ids, BLOCK - 1), BLOCK).astype(BF16)
        looked = jnp.dot(table, low_hot, preferred_element_type=F32)
        row_hot = one_hot(lax.shift_right_logical(ids, 7), set_rows)
        upper = jnp.sum(looked[:set_rows] * row_hot, axis=0, keepdims=True)
        lower = jnp.sum(looked[set_rows:] * row_hot, axis=0, keepdims=True)
        lanes = slice(b * BLOCK, (b + 1) * BLOCK)
        member[:, lanes] = one_hot(lower.astype(jnp.int32), span).astype(BF16)
        spread = jnp.broadcast_to(upper, (scen_dev, BLOCK))
        for e in range(couples):
            pair_mask[e * scen_dev : (e + 1) * scen_dev, lanes] = jnp.where(
                spread == float(e), 1.0, 0.0
            ).astype(BF16)

    for copy in move_copies:
        copy.wait()

    for b in range(trade_blocks):
        picked = jnp.concatenate(
            [moves[delta_index[k, b]] for k in range(per_block)], axis=1
        )
        block = delta_tiles[b * per_block : (b + 1) * per_block].reshape(
            per_block * BLOCK, BLOCK
        )
        value = jnp.dot(picked, block, preferred_element_type=F32) + base[b : b + 1, :]
        first = value.astype(BF16)
        second = (value - first.astype(F32)).astype(BF16)
        lanes = slice(b * BLOCK, (b + 1) * BLOCK)
        for e in range(couples):
            mask = pair_mask[e * scen_dev : (e + 1) * scen_dev, lanes]
            row = (e % half) * scen_dev
            spread_values[e // half, row : row + scen_dev, lanes] = first * mask
            row += half * scen_dev
            spread_values[e // half, row : row + scen_dev, lanes] = second * mask
    swaps = []
    for step in range(2):
        netted = lax.dot_general(
            spread_values[1 - near if step == 0 else near],
            member[...],
            (((1,), (1,)), ((), ())),
            preferred_element_type=F32,
        )
        netted = netted[: half * scen_dev] + netted[half * scen_dev :]
        for j in range(half):
            rows = slice(j * scen_dev, (j + 1) * scen_dev)
            partial[0, step, j] = netted[rows, :own_sets]
            partial[1, step, j] = netted[rows, own_sets:]
        swap = pltpu.make_async_remote_copy(
            src_ref=partial.at[1 - parity, step],
            dst_ref=got_pair.at[step],
            send_sem=pair_send.at[step],
            recv_sem=pair_recv.at[step],
            device_id={"wide": partner},
            device_id_type=MESH,
        )
        swap.start()
        swaps.append(swap)

    wide_copies = []
    for step in range(2):
        swaps[step].wait()
        halved[step] = partial[parity, step] + got_pair[step]
        for k, (when, start, j) in enumerate(targets):
            if when == step:
                copy = pltpu.make_async_remote_copy(
                    src_ref=halved.at[step, j],
                    dst_ref=got_wide.at[k],
                    send_sem=wide_send.at[k],
                    recv_sem=wide_recv.at[k],
                    device_id={"wide": (start + j) * 2 + parity},
                    device_id_type=MESH,
                )
                copy.start()
                wide_copies.append(copy)
    total = halved[1, place]
    for k in range(len(targets) - 1, -1, -1):
        wide_copies[k].wait()
        total += got_wide[k]

    exposure = jnp.maximum(total, 0.0)
    hit = jnp.where(default_step[...] == STEP, exposure, 0.0)
    sums[group, 0:1] = jnp.sum(exposure, axis=0, keepdims=True)
    sums[group, 1:2] = jnp.sum(hit, axis=0, keepdims=True)
    sum_copies = [
        pltpu.make_async_remote_copy(
            src_ref=sums.at[group],
            dst_ref=sums.at[group],
            send_sem=sum_send.at[k],
            recv_sem=sum_recv.at[k],
            device_id={"narrow": peer},
            device_id_type=MESH,
        )
        for k, peer in enumerate(narrow_peers)
    ]
    for copy in sum_copies:
        copy.start()
    for copy in sum_copies:
        copy.wait()
    both = sums[0]
    for n in range(1, narrow_count):
        both += sums[n]
    sums_out[...] = both


def on_device(
    shocks,
    load_tiles,
    load_index,
    delta_tiles,
    delta_index,
    base_value,
    trade_set,
    set_slot,
    default_step,
):
    narrow_count = lax.axis_size("narrow")
    wide_count = lax.axis_size("wide")
    scen_all, width = shocks.shape
    factor_blocks = width // BLOCK
    own_blocks = factor_blocks // narrow_count
    scen_dev, own_sets = default_step.shape
    trades = trade_set.shape[0]
    couples = wide_count // 2
    lines = couples * scen_dev
    dma = pltpu.SemaphoreType.DMA
    arrays = (
        shocks,
        load_tiles,
        load_index.T,
        delta_tiles,
        delta_index.T,
        base_value.reshape(-1, BLOCK),
        trade_set.reshape(-1, BLOCK),
        set_slot.reshape(-1, BLOCK),
        default_step,
    )
    spaces = [pltpu.VMEM, pltpu.VMEM, pltpu.SMEM, pltpu.VMEM, pltpu.SMEM] + [pltpu.VMEM] * 4
    totals = pl.pallas_call(
        functools.partial(kernel, narrow_count, wide_count),
        out_shape=jax.ShapeDtypeStruct((2, own_sets), F32),
        in_specs=[pl.BlockSpec(memory_space=pl.ANY)] * len(arrays),
        out_specs=pl.BlockSpec(memory_space=pltpu.VMEM),
        scratch_shapes=[space(array.shape, array.dtype) for space, array in zip(spaces, arrays)]
        + [
            pltpu.VMEM((factor_blocks, scen_all, BLOCK), BF16),
            pltpu.VMEM((narrow_count, own_blocks, scen_dev, BLOCK), BF16),
            pltpu.VMEM((factor_blocks, scen_dev, BLOCK), BF16),
            pltpu.VMEM((load_tiles.shape[0], scen_all, BLOCK), F32),
            pltpu.VMEM((2 * own_sets, trades), BF16),
            pltpu.VMEM((lines, trades), BF16),
            pltpu.VMEM((2, lines, trades), BF16),
            pltpu.VMEM((2, 2, couples // 2, scen_dev, own_sets), F32),
            pltpu.VMEM((2, couples // 2, scen_dev, own_sets), F32),
            pltpu.VMEM((2, couples // 2, scen_dev, own_sets), F32),
            pltpu.VMEM((couples - 1, scen_dev, own_sets), F32),
            pltpu.VMEM((narrow_count, 2, own_sets), F32),
            dma((len(arrays),)),
            dma((narrow_count - 1,)),
            dma((narrow_count - 1,)),
            dma((2,)),
            dma((2,)),
            dma((couples - 1,)),
            dma((couples - 1,)),
            dma((narrow_count - 1,)),
            dma((narrow_count - 1,)),
        ],
        compiler_params=pltpu.CompilerParams(collective_id=0, has_side_effects=True),
    )(*arrays)
    return totals[0] / scen_all, totals[1] * (STEPS / scen_all)


def solution(mesh):
    return jax.shard_map(
        on_device,
        mesh=mesh,
        in_specs=(
            P(),
            P("narrow", None, None),
            P("narrow", None),
            P("wide", None, None),
            P("wide", None),
            P("wide"),
            P("wide"),
            P(),
            P("narrow", "wide"),
        ),
        out_specs=(P("wide"), P("wide")),
        check_vma=False,
    )
```

time: 26.7 us -> 23.8 us (0.89)
  local copies, waits for them, and re-layouts: 5.01 us -> 0 us
  other arithmetic: 0 us -> 1.25 us
  Pallas kernels: 20.8 us -> 21.7 us
    unnamed x4 -> x0, local copies, waits for them, and re-layouts: 5.01 us -> none
    mul x0 -> x1, other arithmetic: none -> 1.25 us  [on_device(): return (totals[0] / scen_all, totals[1] * (STEPS / scen_all))]
    pallas_call x1, Pallas kernels: 20.8 us -> 21.7 us  [on_device(): pl.pallas_call(functools.partial(kernel, narrow_count, wide_count), out_s...]
where the time goes in v2:
time: 23.8 us; the launch traced here: 23.6 us
  Pallas kernels  21.7 us (91%)
  other arithmetic  1.25 us (5%)
  between operations  0.64 us (3%)
    pallas_call x1, Pallas kernels, on_device(): pl.pallas_call(functools.partial(kernel, narrow_count, wide_count), out_s...  21.7 us
    mul x1, other arithmetic, on_device(): return (totals[0] / scen_all, totals[1] * (STEPS / scen_all))  1.25 us

profile of v2, /device:TPU:0, one launch (start us, length us, event | category | flops | bytes accessed | tf_op | source)
XLA Modules:
  0.0 23.6 jit_solution(9296068256697951276)
XLA Ops:
  0.6 21.7 %shard_map.104 = f32[2,128]{1,0:T(2,128)} custom-call(bf16[64,4096]{1,0:T(8,128)(2,1)} %shocks_hbm.1, bf16[16,128,128]{2,1,0:T(8,128)(2,1)} %load_tiles_hbm.1, s32[2,16]{1,0:T(2,128)} %bitcast.13, bf16[64,128,128]{2,1,0:T(8,128)(2,1)} %delta_tiles_hbm.1, s32[4,16]{1,0:T(4,128)} %bitcast.12, f32[16,128]{1,0:T(8,128)} %bitcast.9, s32[16,128]{1,0:T(8,128)} %bitcast.10, ...), custom_call_target="tpu_custom_call" | custom-call | tf_op jit(solution)/shard_map/pallas_call | solution.py:294
  22.3 1.3 %multiply_bitcast_fusion = (f32[128]{0:T(128)}, f32[128]{0:T(128)}) fusion(f32[2,128]{1,0:T(2,128)} %shard_map.104), kind=kLoop, calls=%fused_computation | loop fusion | flops 256 | bytes 2048 | tf_op jit(solution)/shard_map/mul | solution.py:325

commit v3 on v2

--- a/solution.py
+++ b/solution.py
@@ -293,7 +293,7 @@
     spaces = [pltpu.VMEM, pltpu.VMEM, pltpu.SMEM, pltpu.VMEM, pltpu.SMEM] + [pltpu.VMEM] * 4
     totals = pl.pallas_call(
         functools.partial(kernel, narrow_count, wide_count),
-        out_shape=jax.ShapeDtypeStruct((2, own_sets), F32),
+        out_shape=pltpu.VMEM((2, own_sets), F32),
         in_specs=[pl.BlockSpec(memory_space=pl.ANY)] * len(arrays),
         out_specs=pl.BlockSpec(memory_space=pltpu.VMEM),
         scratch_shapes=[space(array.shape, array.dtype) for space, array in zip(spaces, arrays)]

time: 23.8 us -> 22.4 us (0.941)
  other arithmetic: 1.25 us -> 0.52 us
  Pallas kernels: 21.7 us -> 21.1 us
    mul x1, other arithmetic: 1.25 us -> 0.52 us  [on_device(): return (totals[0] / scen_all, totals[1] * (STEPS / scen_all))]
    pallas_call x1, Pallas kernels: 21.7 us -> 21.1 us  [on_device(): pl.pallas_call(functools.partial(kernel, narrow_count, wide_count), out_s...]
where the time goes in v3:
time: 22.4 us; the launch traced here: 22.3 us
  Pallas kernels  21.1 us (94%)
  between operations  0.64 us (3%)
  other arithmetic  0.52 us (2%)
    pallas_call x1, Pallas kernels, on_device(): pl.pallas_call(functools.partial(kernel, narrow_count, wide_count), out_s...  21.1 us
    mul x1, other arithmetic, on_device(): return (totals[0] / scen_all, totals[1] * (STEPS / scen_all))  0.52 us

profile of v3, /device:TPU:0, one launch (start us, length us, event | category | flops | bytes accessed | tf_op | source)
XLA Modules:
  0.0 22.3 jit_solution(2447847723531958922)
XLA Ops:
  0.6 21.1 %shard_map.104 = f32[2,128]{1,0:T(2,128)S(1)} custom-call(bf16[64,4096]{1,0:T(8,128)(2,1)} %shocks_hbm.1, bf16[16,128,128]{2,1,0:T(8,128)(2,1)} %load_tiles_hbm.1, s32[2,16]{1,0:T(2,128)} %bitcast.13, bf16[64,128,128]{2,1,0:T(8,128)(2,1)} %delta_tiles_hbm.1, s32[4,16]{1,0:T(4,128)} %bitcast.12, f32[16,128]{1,0:T(8,128)} %bitcast.9, s32[16,128]{1,0:T(8,128)} %bitcast.10, ...), custom_call_target="tpu_custom_call" | custom-call | tf_op jit(solution)/shard_map/pallas_call | solution.py:294
  21.8 0.5 %multiply_bitcast_fusion = (f32[128]{0:T(128)}, f32[128]{0:T(128)}) fusion(f32[2,128]{1,0:T(2,128)S(1)} %shard_map.104), kind=kLoop, calls=%fused_computation | loop fusion | flops 256 | bytes 2048 | tf_op jit(solution)/shard_map/mul | solution.py:325
